TPU v7x, 32 devices: a whole 2x2x4 slice. The times are simulated.
32 devices in a mesh: blk: 4 (over y, core), group: 8 (over z, x).
Axes of the slice: x: 2, y: 2, z: 4, core: 2. Of those that a mesh axis runs over, the one named last changes fastest.
Arguments:
- queries: bfloat16 [32, 16, 128], P(('blk', 'group')), may hold values from -2.5 to 2.5
- query_mask: int32 [32, 16], P(('blk', 'group')), may hold values from 0 to 1, as said below
- positive: int32 [32], P(('blk', 'group')), may hold values from 0 to 63
- page_vectors: bfloat16 [64, 128, 128], P(('blk', 'group')), may hold values from -2 to 2
- page_mask: int32 [64, 128], P(('blk', 'group')), may hold values from 0 to 1, as said below
Outputs:
- grad_queries: float32 [32, 16, 128], P(('blk', 'group'))
- grad_pages: float32 [64, 128, 128], P(('blk', 'group'))
- mean_loss: float32 [], replicated
Inputs may be any that keep to these rules, and one draw needn't show every extreme that they name: `query_mask`: each row holds ones on its first 8 to 16 token slots and zeros after them. `page_mask`: each row holds ones on its first 32 to 128 patch slots and zeros after them.
All inputs are finite; a program needn't handle non-finite values.
Results may differ from a plain program's by a relative error of at most 0.0028.
Values may be sent and summed in bfloat16 or wider, within the bound.
No kernel may reach another device: no remote copies, remote signals or barrier semaphores. Data moves between devices by JAX's collectives and lax.ppermute only.
A program may use at most 64 MiB of HBM per device.

v0:
```python
import math
import jax
import jax.numpy as jnp
from jax import lax
from jax.sharding import PartitionSpec as P

relaxation_scale_factor = 0.5
guarded_floor_entry = -1e30


def combined_all(part, axis, combine):
    gathered = jax.tree.map(lambda a: lax.all_gather(a, axis), part)

    def take(source):
        return jax.tree.map(lambda a: lax.dynamic_index_in_dim(a, source, 0, False), gathered)

    return lax.fori_loop(
        1, lax.axis_size(axis), lambda source, state: combine(state, take(source)), take(0)
    )


def from_behind(value, axis, steps):
    count = lax.axis_size(axis)
    pairs = [(source, (source + steps) % count) for source in range(count)]
    return lax.ppermute(value, axis, pairs)


def masked_logits(row_block, lone_document, live_image_embeddings):
    similarity_matrix = lax.dot_general(
        row_block, lone_document, (((1,), (1,)), ((), ())), preferred_element_type=jnp.float32
    )
    return jnp.where(
        live_image_embeddings[None, :] > 0,
        similarity_matrix / relaxation_scale_factor,
        guarded_floor_entry,
    )


def combine_parts(earlier, later):
    highest = jnp.maximum(earlier[0], later[0])
    totals = earlier[1] * jnp.exp(earlier[0] - highest) + later[1] * jnp.exp(later[0] - highest)
    return (highest, totals, earlier[2] + later[2])


def on_device(queries, query_mask, positive, page_vectors, page_mask):
    tokens = queries.shape[1]
    features = queries.shape[2]
    local_pages = page_vectors.shape[0]
    blocks = lax.axis_size("blk")
    members = lax.axis_size("group")
    bundle_size = queries.shape[0] * members
    total_queries = bundle_size * blocks
    natural_logarithm_lengths = jnp.log(jnp.sum(page_mask.astype(jnp.float32), axis=1))
    bundle_vectors, bundle_masks, bundle_targets = (
        lax.all_gather(queries, "group", axis=0, tiled=True),
        lax.all_gather(query_mask, "group", axis=0, tiled=True),
        lax.all_gather(positive, "group", axis=0, tiled=True),
    )

    def forward_piece(folded, shard_in, root_row):
        scores, lse_rows, live_all, owners, kept = folded
        vectors, token_masks, targets = shard_in
        amount = vectors.shape[0]
        stride = math.gcd(amount, max(1, 512 // tokens))

        def run_block(number, current):
            scores, lse_rows = current
            offset = number * stride
            slab_rows = lax.dynamic_slice_in_dim(vectors, offset, stride, 0).reshape(
                stride * tokens, features
            )
            alive = lax.dynamic_slice_in_dim(token_masks, offset, stride, 0).astype(jnp.float32)
            found_sums = []
            for index_page in range(local_pages):
                masked = masked_logits(slab_rows, page_vectors[index_page], page_mask[index_page])
                highest = jnp.max(masked, axis=1, keepdims=True)
                found_sums.append(
                    highest[:, 0] + jnp.log(jnp.sum(jnp.exp(masked - highest), axis=1))
                )
            logsumexp_results = jnp.stack(found_sums, axis=1).reshape(stride, tokens, local_pages)
            softened_supremum = relaxation_scale_factor * (
                logsumexp_results - natural_logarithm_lengths
            )
            page_score = jnp.sum(alive[:, :, None] * softened_supremum, axis=1)
            scores = lax.dynamic_update_slice_in_dim(scores, page_score, offset, 0)
            lse_rows = lax.dynamic_update_slice_in_dim(lse_rows, logsumexp_results, offset, 0)
            return (scores, lse_rows)

        scores, lse_rows = lax.fori_loop(0, amount // stride, run_block, (scores, lse_rows))
        live_all = lax.dynamic_update_slice_in_dim(live_all, token_masks, root_row, 0)
        owners = lax.dynamic_update_slice_in_dim(owners, targets, root_row, 0)
        kept = vectors
        return (scores, lse_rows, live_all, owners, kept)

    starting = (
        jnp.zeros((total_queries, local_pages), jnp.float32),
        jnp.zeros((total_queries, tokens, local_pages), jnp.float32),
        jnp.zeros((total_queries, tokens), jnp.int32),
        jnp.zeros((total_queries,), jnp.int32),
        jnp.zeros((total_queries, tokens, features), jnp.bfloat16),
    )
    scores, lse_rows, live_all, owners, kept = forward_piece(
        starting,
        (
            lax.all_gather(bundle_vectors, "blk", axis=0, tiled=True),
            lax.all_gather(bundle_masks, "blk", axis=0, tiled=True),
            lax.all_gather(bundle_targets, "blk", axis=0, tiled=True),
        ),
        jnp.int32(0),
    )
    position = lax.axis_index(("blk", "group"))
    page_ids = position * local_pages + jnp.arange(local_pages, dtype=jnp.int32)
    chosen = owners[:, None] == page_ids[None, :]
    picked_local = jnp.sum(jnp.where(chosen, scores, 0.0))
    local_top = jnp.max(scores, axis=1)
    local_total = jnp.sum(jnp.exp(scores - local_top[:, None]), axis=1)
    highest, totals, picked = combined_all(
        (local_top, local_total, picked_local), ("blk", "group"), combine_parts
    )
    page_lse = highest + jnp.log(totals)
    mean_loss = (jnp.sum(page_lse) - picked) / total_queries
    coefficient = jnp.exp(scores - page_lse[:, None]) - chosen.astype(jnp.float32)
    factor_scale = coefficient[:, None, :] * live_all.astype(jnp.float32)[:, :, None]

    def slice_rows(root_row, amount):
        sums = lax.dynamic_slice_in_dim(lse_rows, root_row, amount, 0).reshape(
            amount * tokens, local_pages
        )
        scales = lax.dynamic_slice_in_dim(factor_scale, root_row, amount, 0).reshape(
            amount * tokens, local_pages
        )
        return (sums, scales)

    def gradient_terms(row_block, logsumexp_results, scales, page_grads):
        partial_value = jnp.zeros(row_block.shape, jnp.float32)
        for number in range(local_pages):
            masked = masked_logits(row_block, page_vectors[number], page_mask[number])
            weights = jnp.exp(masked - logsumexp_results[:, number : number + 1])
            factor = (scales[:, number : number + 1] * weights).astype(jnp.bfloat16)
            partial_value = partial_value + jnp.dot(
                factor, page_vectors[number], preferred_element_type=jnp.float32
            )
            update = lax.dot_general(
                factor, row_block, (((0,), (0,)), ((), ())), preferred_element_type=jnp.float32
            )
            page_grads = page_grads.at[number].add(update)
        return (partial_value, page_grads)

    home = lax.axis_index("blk")
    page_grads = jnp.zeros(page_vectors.shape, jnp.float32)

    def visit_one(moving, collected, page_grads, lap_index):
        root_row = (home - lap_index) % blocks * bundle_size
        sums, scales = slice_rows(root_row, bundle_size)
        partial_value, page_grads = gradient_terms(
            moving.reshape(bundle_size * tokens, features), sums, scales, page_grads
        )
        return (collected + partial_value.reshape(bundle_size, tokens, features), page_grads)

    def pass_one(collected):
        return from_behind(collected, "blk", 1)

    def turn_one(lap_index, current):
        moving, collected, page_grads = current
        collected, page_grads = visit_one(moving, collected, page_grads, lap_index)
        moving = from_behind(moving, "blk", 1)
        return (moving, pass_one(collected), page_grads)

    empty_whole = jnp.zeros((bundle_size, tokens, features), jnp.float32)
    moving, collected, page_grads = lax.fori_loop(
        0, blocks - 1, turn_one, (bundle_vectors, empty_whole, page_grads)
    )
    collected, page_grads = visit_one(moving, collected, page_grads, blocks - 1)
    collected = pass_one(collected)
    grad_queries = lax.psum_scatter(collected, "group", scatter_dimension=0, tiled=True)
    return (grad_queries, page_grads, mean_loss)


def solution(mesh):
    in_specs = (
        P(("blk", "group"), None, None),
        P(("blk", "group"), None),
        P(("blk", "group")),
        P(("blk", "group"), None, None),
        P(("blk", "group"), None),
    )
    out_specs = (P(("blk", "group"), None, None), P(("blk", "group"), None, None), P())
    return jax.shard_map(
        on_device, mesh=mesh, in_specs=in_specs, out_specs=out_specs, check_vma=False
    )
```

profile of v0, /device:TPU:0, one launch (start us, length us, event | category | flops | bytes accessed | tf_op | source)
XLA Modules:
  0.0 262.9 jit_solution(15310981650806206361)
XLA Ops:
  7.2 0.8 compare_bitcast_fusion.2
  8.1 32.4 %all_gather.36 = bf16[8,16,128]{2,1,0:T(8,128)(2,1)S(1)} all-gather(bf16[1,16,128]{2,1,0:T(8,128)(2,1)S(1)} %copy-done.4), channel_id=1, replica_groups=mesh['blk'=4,'group'=8] {'group'}, dimensions={0}, use_global_device_ids=true | all-gather | bytes 36864 | tf_op jit(solution)/shard_map/all_gather | solution.py:55
  40.6 5.5 %all_gather.37 = bf16[32,16,128]{2,1,0:T(8,128)(2,1)S(1)} all-gather(bf16[8,16,128]{2,1,0:T(8,128)(2,1)S(1)} %all_gather.36), channel_id=1, replica_groups=mesh['blk'=4,'group'=8] {'blk'}, dimensions={0}, use_global_device_ids=true | all-gather | bytes 163840 | tf_op jit(solution)/shard_map/all_gather | solution.py:105
  46.8 0.7 copy-done.5
  47.5 20.4 %all-gather.2 = s32[8,1,16]{2,1,0:T(1,128)S(1)} all-gather(s32[1,1,16]{2,1,0:T(1,128)S(1)} %bitcast.182), channel_id=1, replica_groups=mesh['blk'=4,'group'=8] {'group'}, dimensions={0}, use_global_device_ids=true | all-gather | bytes 576 | tf_op jit(solution)/shard_map/all_gather | solution.py:56
  67.9 5.2 %all_gather.39 = s32[32,16]{1,0:T(8,128)S(1)} all-gather(s32[8,16]{1,0:T(8,128)S(1)} %bitcast.181), channel_id=1, replica_groups=mesh['blk'=4,'group'=8] {'blk'}, dimensions={0}, use_global_device_ids=true | all-gather | bytes 2560 | tf_op jit(solution)/shard_map/all_gather | solution.py:106
  73.1 0.7 copy-done.7
  75.0 0.8 dynamic-update-slice.28
  75.8 6.8 %all-reduce.2 = s32[8]{0:T(128)S(1)} all-reduce(s32[8]{0:T(128)S(1)} %dynamic-update-slice.28), channel_id=1, replica_groups=mesh['blk'=4,'group'=8] {'group'}, use_global_device_ids=true, to_apply=%add.2 | all-reduce | flops 8 | bytes 64
  84.1 4.9 %all-reduce.3 = s32[32]{0:T(128)S(1)} all-reduce(s32[32]{0:T(128)S(1)} %dynamic-update-slice.29), channel_id=1, replica_groups=mesh['blk'=4,'group'=8] {'blk'}, use_global_device_ids=true, to_apply=%add.3 | all-reduce | flops 32 | bytes 256
  89.2 0.7 fusion.54
  90.3 0.8 dynamic-update-slice.30
  91.0 40.5 %all-reduce.5 = (f32[1024]{0:T(1024)S(1)}, f32[1024]{0:T(1024)S(1)}, f32[32]{0:T(128)S(1)}) all-reduce(f32[1024]{0:T(1024)S(1)} %dynamic-update-slice.26, f32[1024]{0:T(1024)S(1)} %dynamic-update-slice.27, f32[32]{0:T(128)S(1)} %dynamic-update-slice.30), channel_id=2, replica_groups=mesh['blk'=4,'group'=8] {'blk','group'}, use_global_device_ids=true, to_apply=%add | all-reduce | flops 2080 | bytes 16640
  131.7 39.9 %while.48 = (s32[]{:T(128)}, f32[32]{0:T(128)S(1)}, f32[32]{0:T(128)S(1)}, f32[]{:T(128)}, f32[32,32]{1,0:T(8,128)S(1)}, /*index=5*/f32[32,32]{1,0:T(8,128)S(1)}, f32[32]{0:T(128)S(1)}, s32[]{:T(128)}, s32[]{:T(128)}, s32[]{:T(128)}) while((s32[]{:T(128)}, f32[32]{0:T(128)S(1)}, f32[32]{0:T(128)S(1)}, f32[]{:T(128)}, ...), condition=%wide.region_10.11_spmd, body=%wide.region_9.10_spmd.sunk | while | flops 198 | bytes 939 | solution.py:17
  131.7 0.6 dynamic_slice.91
  133.0 0.6 dynamic_slice.91
  134.3 0.6 dynamic_slice.91
  135.6 0.6 dynamic_slice.91
  145.9 0.6 dynamic_slice.91
  147.2 0.6 dynamic_slice.91
  170.4 0.6 dynamic_slice.91
  171.6 0.6 fusion.56
  172.6 13.9 %while.49 = (s32[]{:T(128)}, bf16[8,16,128]{2,1,0:T(8,128)(2,1)S(1)}, f32[8,16,128]{2,1,0:T(8,128)S(1)}, f32[2,128,128]{2,1,0:T(8,128)S(1)}, s32[]{:T(128)}, /*i...) while((s32[]{:T(128)}, ...), condition=%wide.region_12.13_spmd, body=%wide.region_11.12_spmd.sunk | while | flops 25395472 | bytes 1589896 | solution.py:170
  173.6 2.4 collective-permute-start.1
  176.4 0.9 collective-permute-done.1
  178.2 2.4 collective-permute-start.1
  181.0 0.9 collective-permute-done.1
  182.8 2.4 collective-permute-start.1
  185.6 0.9 collective-permute-done.1
  188.1 2.8 %collective-permute-done.2 = f32[8,16,128]{2,1,0:T(8,128)S(1)} collective-permute-done((f32[8,16,128]{2,1,0:T(8,128)S(1)}, f32[8,16,128]{2,1,0:T(8,128)S(1)}, u32[]{:S(2)}, u32[]{:S(2)}) %collective-permute-start.2) | collective-permute-done | bytes 65568 | tf_op jit(solution)/shard_map/ppermute | solution.py:25
  190.9 0.6 copy-done.2
  191.8 63.1 %reduce-scatter.2.cloned.1.call-done = f32[1,16,128]{2,1,0:T(8,128)} async-done(((f32[8,16,128]{2,1,0:T(8,128)}), f32[1,16,128]{2,1,0:T(8,128)}) %reduce-scatter.2.cloned.1.call-update) | async-done | bytes 8208 | tf_op jit(solution)/shard_map/reduce_scatter | solution.py:175
  (166 shorter events, 23.0 us)
Async XLA Ops:
  7.2 0.8 copy-start.3
  7.2 0.9 copy-start.4
  7.2 247.7 %reduce-scatter.2.cloned.1.call-start = ((), (), s32[]{:S(2)}) async-start(), calls=%async_computation.1 | async-start | bytes 73728 | tf_op jit(solution)/shard_map/reduce_scatter | solution.py:175
  40.5 5.5 %copy-start.1 = (bf16[2,128,128]{2,1,0:T(8,128)(2,1)S(1)}, bf16[2,128,128]{2,1,0:T(8,128)(2,1)}, u32[]{:S(2)}) copy-start(bf16[2,128,128]{2,1,0:T(8,128)(2,1)} %param.20) | copy-start | bytes 196612
  46.8 0.7 copy-start.5
  73.1 0.7 copy-start.7
  75.8 6.8 %copy-start.6 = (u32[32]{0:T(128)S(1)}, u32[32]{0:T(128)}, u32[]{:S(2)}) copy-start(u32[32]{0:T(128)} %constant.385) | copy-start | bytes 388
  172.6 3.7 %collective-permute-start = (bf16[8,16,128]{2,1,0:T(8,128)(2,1)S(1)}, bf16[8,16,128]{2,1,0:T(8,128)(2,1)S(1)}, u32[]{:S(2)}, u32[]{:S(2)}) collective-permute-start(bf16[8,16,128]{2,1,0:T(8,128)(2,1)S(1)} %copy.33), channel_id=1, source_target_pairs={{0,8},{8,16},{16,24},{24,0},{1,9},{9,17},{17,25},{25,1},{2,10},{10... | collective-permute-start | bytes 98312 | tf_op jit(solution)/shard_map/while/body/eval_jaxpr/ppermute | solution.py:25
  173.6 3.7 %collective-permute-start.1 = (f32[8,16,128]{2,1,0:T(8,128)S(1)}, f32[8,16,128]{2,1,0:T(8,128)S(1)}, u32[]{:S(2)}, u32[]{:S(2)}) collective-permute-start(f32[8,16,128]{2,1,0:T(8,128)S(1)} %add.305), channel_id=1, source_target_pairs={{0,8},{8,16},{16,24},{24,0},{1,9},{9,17},{17,25},{25,1},{2,10},{10... | collective-permute-start | bytes 196616 | tf_op jit(solution)/shard_map/while/body/eval_jaxpr/ppermute | solution.py:25
  177.3 3.7 %collective-permute-start = (bf16[8,16,128]{2,1,0:T(8,128)(2,1)S(1)}, bf16[8,16,128]{2,1,0:T(8,128)(2,1)S(1)}, u32[]{:S(2)}, u32[]{:S(2)}) collective-permute-start(bf16[8,16,128]{2,1,0:T(8,128)(2,1)S(1)} %copy.33), channel_id=1, source_target_pairs={{0,8},{8,16},{16,24},{24,0},{1,9},{9,17},{17,25},{25,1},{2,10},{10... | collective-permute-start | bytes 98312 | tf_op jit(solution)/shard_map/while/body/eval_jaxpr/ppermute | solution.py:25
  178.2 3.7 %collective-permute-start.1 = (f32[8,16,128]{2,1,0:T(8,128)S(1)}, f32[8,16,128]{2,1,0:T(8,128)S(1)}, u32[]{:S(2)}, u32[]{:S(2)}) collective-permute-start(f32[8,16,128]{2,1,0:T(8,128)S(1)} %add.305), channel_id=1, source_target_pairs={{0,8},{8,16},{16,24},{24,0},{1,9},{9,17},{17,25},{25,1},{2,10},{10... | collective-permute-start | bytes 196616 | tf_op jit(solution)/shard_map/while/body/eval_jaxpr/ppermute | solution.py:25
  182.0 3.6 %collective-permute-start = (bf16[8,16,128]{2,1,0:T(8,128)(2,1)S(1)}, bf16[8,16,128]{2,1,0:T(8,128)(2,1)S(1)}, u32[]{:S(2)}, u32[]{:S(2)}) collective-permute-start(bf16[8,16,128]{2,1,0:T(8,128)(2,1)S(1)} %copy.33), channel_id=1, source_target_pairs={{0,8},{8,16},{16,24},{24,0},{1,9},{9,17},{17,25},{25,1},{2,10},{10... | collective-permute-start | bytes 98312 | tf_op jit(solution)/shard_map/while/body/eval_jaxpr/ppermute | solution.py:25
  182.8 3.7 %collective-permute-start.1 = (f32[8,16,128]{2,1,0:T(8,128)S(1)}, f32[8,16,128]{2,1,0:T(8,128)S(1)}, u32[]{:S(2)}, u32[]{:S(2)}) collective-permute-start(f32[8,16,128]{2,1,0:T(8,128)S(1)} %add.305), channel_id=1, source_target_pairs={{0,8},{8,16},{16,24},{24,0},{1,9},{9,17},{17,25},{25,1},{2,10},{10... | collective-permute-start | bytes 196616 | tf_op jit(solution)/shard_map/while/body/eval_jaxpr/ppermute | solution.py:25
  187.2 3.7 %collective-permute-start.2 = (f32[8,16,128]{2,1,0:T(8,128)S(1)}, f32[8,16,128]{2,1,0:T(8,128)S(1)}, u32[]{:S(2)}, u32[]{:S(2)}) collective-permute-start(f32[8,16,128]{2,1,0:T(8,128)S(1)} %add.250), channel_id=1, source_target_pairs={{0,8},{8,16},{16,24},{24,0},{1,9},{9,17},{17,25},{25,1},{2,10},{10... | collective-permute-start | bytes 196616 | tf_op jit(solution)/shard_map/ppermute | solution.py:25
  190.9 0.6 copy-start.2
  191.8 63.1 %copy-start = (f32[2,128,128]{2,1,0:T(8,128)}, f32[2,128,128]{2,1,0:T(8,128)S(1)}, u32[]{:S(2)}) copy-start(f32[2,128,128]{2,1,0:T(8,128)S(1)} %fusion.38) | copy-start | bytes 393220
Sparse Core Ops, SparseCore 0:
  191.7 63.1 reduce-scatter.1
where the time goes:
time: 264 us; the launch traced here: 263 us
  blocking collectives  116 us (44%)
  waiting for transfers between devices  68.8 us (26%)
  local copies, waits for them, and re-layouts  24.5 us (9%)
  loops' own time  21.1 us (8%)
  between operations  17.3 us (7%)
  starting transfers between devices  7.44 us (3%)
  matrix products  4.3 us (2%)
  other arithmetic  3.58 us (1%)
    reduce_scatter x1, waiting for transfers between devices, on_device(): lax.psum_scatter(collected, 'group', scatter_dimension=0, tiled=True)  63.1 us
    unnamed x3, blocking collectives  52.2 us
    all_gather x1, blocking collectives, on_device(): lax.all_gather(queries, 'group', axis=0, tiled=True)  32.4 us
    another operation x1, loops' own time, combined_all(): lax.fori_loop(1, lax.axis_size(axis), lambda source, state: combine(state...  20.9 us
    all_gather x1, blocking collectives, on_device(): lax.all_gather(query_mask, 'group', axis=0, tiled=True)  20.4 us
    dynamic_slice x33, local copies, waits for them, and re-layouts, take(): lax.dynamic_index_in_dim(a, source, 0, False)  18.2 us
    ppermute x7, starting transfers between devices, from_behind(): return lax.ppermute(value, axis, pairs)  7.4 us
    ppermute x7, waiting for transfers between devices, from_behind(): return lax.ppermute(value, axis, pairs)  5.66 us
  transfers between devices with their start and end apart: 8, of which 5 were waited for; matrix products, arithmetic and copies ran while one was open for 1% of the time, Pallas kernels for 0%

commit v1 on v0

--- a/solution.py
+++ b/solution.py
@@ -51,9 +51,26 @@
     bundle_size = queries.shape[0] * members
     total_queries = bundle_size * blocks
     natural_logarithm_lengths = jnp.log(jnp.sum(page_mask.astype(jnp.float32), axis=1))
+
+    def _create_ways(body):
+        xs_all = [body]
+        j = 1
+        how_many = lax.axis_size("group")
+        while j < how_many:
+            xs_all.append(
+                lax.ppermute(
+                    xs_all[j - 1],
+                    axis_name="group",
+                    perm=[(dev, (dev - 1) % how_many) for dev in range(how_many)],
+                )
+            )
+            j = j + 1
+        fresh = jnp.concatenate(xs_all, 0)
+        return jnp.roll(fresh, lax.axis_index("group") * body.shape[0], 0)
+
     bundle_vectors, bundle_masks, bundle_targets = (
         lax.all_gather(queries, "group", axis=0, tiled=True),
-        lax.all_gather(query_mask, "group", axis=0, tiled=True),
+        _create_ways(query_mask),
         lax.all_gather(positive, "group", axis=0, tiled=True),
     )
 

time: 264 us -> 285 us (1.080)
  starting transfers between devices: 7.44 us -> 41.1 us
  blocking collectives: 116 us -> 94.6 us
  waiting for transfers between devices: 68.8 us -> 76.9 us
    ppermute x0 -> x7, starting transfers between devices: none -> 33.7 us  [_create_ways(): lax.ppermute(xs_all[j - 1], axis_name='group', perm=[(dev, (dev - 1) % ho...]
    all_gather x1 -> x0, blocking collectives: 20.4 us -> none  [on_device(): lax.all_gather(query_mask, 'group', axis=0, tiled=True)]
    ppermute x0 -> x7, waiting for transfers between devices: none -> 7.77 us  [_create_ways(): lax.ppermute(xs_all[j - 1], axis_name='group', perm=[(dev, (dev - 1) % ho...]
  transfers between devices with their start and end apart: 8 -> 15, of which waited for: 5 -> 11; matrix products, arithmetic and copies ran while one was open for 1% -> 3% of each run, Pallas kernels for 0% -> 0%
where the time goes in v1:
time: 285 us; the launch traced here: 284 us
  blocking collectives  94.6 us (33%)
  waiting for transfers between devices  76.9 us (27%)
  starting transfers between devices  41.1 us (14%)
  local copies, waits for them, and re-layouts  25.5 us (9%)
  loops' own time  21.1 us (7%)
  between operations  17.4 us (6%)
  matrix products  4.31 us (2%)
  other arithmetic  2.96 us (1%)
    reduce_scatter x1, waiting for transfers between devices, on_device(): lax.psum_scatter(collected, 'group', scatter_dimension=0, tiled=True)  63.4 us
    unnamed x3, blocking collectives  53.3 us
    ppermute x7, starting transfers between devices, _create_ways(): lax.ppermute(xs_all[j - 1], axis_name='group', perm=[(dev, (dev - 1) % ho...  33.7 us
    all_gather x1, blocking collectives, on_device(): lax.all_gather(queries, 'group', axis=0, tiled=True)  30.6 us
    another operation x1, loops' own time, combined_all(): lax.fori_loop(1, lax.axis_size(axis), lambda source, state: combine(state...  20.9 us
    dynamic_slice x33, local copies, waits for them, and re-layouts, take(): lax.dynamic_index_in_dim(a, source, 0, False)  18.2 us
    ppermute x7, waiting for transfers between devices, _create_ways(): lax.ppermute(xs_all[j - 1], axis_name='group', perm=[(dev, (dev - 1) % ho...  7.77 us
    ppermute x7, starting transfers between devices, from_behind(): return lax.ppermute(value, axis, pairs)  7.4 us
  transfers between devices with their start and end apart: 15, of which 11 were waited for; matrix products, arithmetic and copies ran while one was open for 3% of the time, Pallas kernels for 0%

profile of v1, /device:TPU:0, one launch (start us, length us, event | category | flops | bytes accessed | tf_op | source)
XLA Modules:
  0.0 283.9 jit_solution(11900771965082065390)
XLA Ops:
  7.2 6.1 %collective-permute-start.2 = (s32[1,16]{1,0:T(1,128)}, s32[1,16]{1,0:T(1,128)S(1)}, u32[]{:S(2)}, u32[]{:S(2)}) collective-permute-start(s32[1,16]{1,0:T(1,128)} %param.18), channel_id=1, source_target_pairs={{0,7},{1,0},{2,1},{3,2},{4,3},{5,4},{6,5},{7,6},{8,15},{9,8},{10,9... | collective-permute-start | bytes 200 | tf_op jit(solution)/shard_map/ppermute | solution.py:61
  14.8 30.6 %all_gather.33 = bf16[8,16,128]{2,1,0:T(8,128)(2,1)S(1)} all-gather(bf16[1,16,128]{2,1,0:T(8,128)(2,1)S(1)} %copy-done.4), channel_id=1, replica_groups=mesh['blk'=4,'group'=8] {'group'}, dimensions={0}, use_global_device_ids=true | all-gather | bytes 36864 | tf_op jit(solution)/shard_map/all_gather | solution.py:72
  45.4 5.5 %all_gather.34 = bf16[32,16,128]{2,1,0:T(8,128)(2,1)S(1)} all-gather(bf16[8,16,128]{2,1,0:T(8,128)(2,1)S(1)} %all_gather.33), channel_id=1, replica_groups=mesh['blk'=4,'group'=8] {'blk'}, dimensions={0}, use_global_device_ids=true | all-gather | bytes 163840 | tf_op jit(solution)/shard_map/all_gather | solution.py:122
  53.7 0.8 dynamic-update-slice.28
  54.5 8.6 %all-reduce.2 = s32[8]{0:T(128)S(1)} all-reduce(s32[8]{0:T(128)S(1)} %dynamic-update-slice.28), channel_id=1, replica_groups=mesh['blk'=4,'group'=8] {'group'}, use_global_device_ids=true, to_apply=%add.2 | all-reduce | flops 8 | bytes 64
  64.7 4.9 %all-reduce.3 = s32[32]{0:T(128)S(1)} all-reduce(s32[32]{0:T(128)S(1)} %dynamic-update-slice.29), channel_id=1, replica_groups=mesh['blk'=4,'group'=8] {'blk'}, use_global_device_ids=true, to_apply=%add.3 | all-reduce | flops 32 | bytes 256
  69.6 2.8 collective-permute-start.3
  72.4 1.3 collective-permute-done.3
  73.7 5.0 %collective-permute-start.4 = (s32[1,16]{1,0:T(1,128)S(1)}, s32[1,16]{1,0:T(1,128)S(1)}, u32[]{:S(2)}, u32[]{:S(2)}) collective-permute-start(s32[1,16]{1,0:T(1,128)S(1)} %collective-permute-done.3), channel_id=1, source_target_pairs={{0,7},{1,0},{2,1},{3,2},{4,3},{5,4},{6,5},{7,6},{8,15},{9,8},{10,9... | collective-permute-start | bytes 200 | tf_op jit(solution)/shard_map/ppermute | solution.py:61
  78.7 1.3 collective-permute-done.4
  79.9 5.0 %collective-permute-start.5 = (s32[1,16]{1,0:T(1,128)S(1)}, s32[1,16]{1,0:T(1,128)S(1)}, u32[]{:S(2)}, u32[]{:S(2)}) collective-permute-start(s32[1,16]{1,0:T(1,128)S(1)} %collective-permute-done.4), channel_id=1, source_target_pairs={{0,7},{1,0},{2,1},{3,2},{4,3},{5,4},{6,5},{7,6},{8,15},{9,8},{10,9... | collective-permute-start | bytes 200 | tf_op jit(solution)/shard_map/ppermute | solution.py:61
  84.9 1.3 collective-permute-done.5
  86.2 5.0 %collective-permute-start.6 = (s32[1,16]{1,0:T(1,128)S(1)}, s32[1,16]{1,0:T(1,128)S(1)}, u32[]{:S(2)}, u32[]{:S(2)}) collective-permute-start(s32[1,16]{1,0:T(1,128)S(1)} %collective-permute-done.5), channel_id=1, source_target_pairs={{0,7},{1,0},{2,1},{3,2},{4,3},{5,4},{6,5},{7,6},{8,15},{9,8},{10,9... | collective-permute-start | bytes 200 | tf_op jit(solution)/shard_map/ppermute | solution.py:61
  91.2 1.3 collective-permute-done.6
  92.5 5.0 %collective-permute-start.7 = (s32[1,16]{1,0:T(1,128)S(1)}, s32[1,16]{1,0:T(1,128)S(1)}, u32[]{:S(2)}, u32[]{:S(2)}) collective-permute-start(s32[1,16]{1,0:T(1,128)S(1)} %collective-permute-done.6), channel_id=1, source_target_pairs={{0,7},{1,0},{2,1},{3,2},{4,3},{5,4},{6,5},{7,6},{8,15},{9,8},{10,9... | collective-permute-start | bytes 200 | tf_op jit(solution)/shard_map/ppermute | solution.py:61
  97.5 1.3 collective-permute-done.7
  98.7 5.0 %collective-permute-start.8 = (s32[1,16]{1,0:T(1,128)S(1)}, s32[1,16]{1,0:T(1,128)S(1)}, u32[]{:S(2)}, u32[]{:S(2)}) collective-permute-start(s32[1,16]{1,0:T(1,128)S(1)} %collective-permute-done.7), channel_id=1, source_target_pairs={{0,7},{1,0},{2,1},{3,2},{4,3},{5,4},{6,5},{7,6},{8,15},{9,8},{10,9... | collective-permute-start | bytes 200 | tf_op jit(solution)/shard_map/ppermute | solution.py:61
  103.7 1.3 collective-permute-done.8
  105.1 5.2 %all_gather.35 = s32[32,16]{1,0:T(8,128)S(1)} all-gather(s32[8,16]{1,0:T(8,128)S(1)} %constant_dynamic-slice_fusion.5), channel_id=1, replica_groups=mesh['blk'=4,'group'=8] {'blk'}, dimensions={0}, use_global_device_ids=true | all-gather | bytes 2560 | tf_op jit(solution)/shard_map/all_gather | solution.py:123
  110.5 0.8 fusion.54
  111.6 0.8 dynamic-update-slice.30
  112.4 39.8 %all-reduce.5 = (f32[1024]{0:T(1024)S(1)}, f32[1024]{0:T(1024)S(1)}, f32[32]{0:T(128)S(1)}) all-reduce(f32[1024]{0:T(1024)S(1)} %dynamic-update-slice.26, f32[1024]{0:T(1024)S(1)} %dynamic-update-slice.27, f32[32]{0:T(128)S(1)} %dynamic-update-slice.30), channel_id=2, replica_groups=mesh['blk'=4,'group'=8] {'blk','group'}, use_global_device_ids=true, to_apply=%add | all-reduce | flops 2080 | bytes 16640
  152.4 40.0 %while.48 = (s32[]{:T(128)}, f32[32]{0:T(128)S(1)}, f32[32]{0:T(128)S(1)}, f32[]{:T(128)}, f32[32,32]{1,0:T(8,128)S(1)}, /*index=5*/f32[32,32]{1,0:T(8,128)S(1)}, f32[32]{0:T(128)S(1)}, s32[]{:T(128)}, s32[]{:T(128)}, s32[]{:T(128)}) while((s32[]{:T(128)}, f32[32]{0:T(128)S(1)}, f32[32]{0:T(128)S(1)}, f32[]{:T(128)}, ...), condition=%wide.region_10.11_spmd, body=%wide.region_9.10_spmd.sunk | while | flops 198 | bytes 939 | solution.py:17
  193.4 13.9 %while.49 = (s32[]{:T(128)}, bf16[8,16,128]{2,1,0:T(8,128)(2,1)S(1)}, f32[8,16,128]{2,1,0:T(8,128)S(1)}, f32[2,128,128]{2,1,0:T(8,128)S(1)}, s32[]{:T(128)}, /*i...) while((s32[]{:T(128)}, ...), condition=%wide.region_12.13_spmd, body=%wide.region_11.12_spmd.sunk | while | flops 25395472 | bytes 1589896 | solution.py:187
  194.3 2.4 collective-permute-start.1
  197.2 0.9 collective-permute-done.1
  199.0 2.4 collective-permute-start.1
  201.8 0.9 collective-permute-done.1
  203.6 2.4 collective-permute-start.1
  206.4 0.9 collective-permute-done.1
  208.9 2.8 collective-permute-done.9
  212.5 63.4 %reduce-scatter.2.cloned.1.call-done = f32[1,16,128]{2,1,0:T(8,128)} async-done(((f32[8,16,128]{2,1,0:T(8,128)}), f32[1,16,128]{2,1,0:T(8,128)}) %reduce-scatter.2.cloned.1.call-update) | async-done | bytes 8208 | tf_op jit(solution)/shard_map/reduce_scatter | solution.py:192
  (181 shorter events, 30.7 us)
Async XLA Ops:
  7.2 268.8 %reduce-scatter.2.cloned.1.call-start = ((), (), s32[]{:S(2)}) async-start(), calls=%async_computation.1 | async-start | bytes 73728 | tf_op jit(solution)/shard_map/reduce_scatter | solution.py:192
  7.2 62.4 %collective-permute-start.2 = (s32[1,16]{1,0:T(1,128)}, s32[1,16]{1,0:T(1,128)S(1)}, u32[]{:S(2)}, u32[]{:S(2)}) collective-permute-start(s32[1,16]{1,0:T(1,128)} %param.18), channel_id=1, source_target_pairs={{0,7},{1,0},{2,1},{3,2},{4,3},{5,4},{6,5},{7,6},{8,15},{9,8},{10,9... | collective-permute-start | bytes 200 | tf_op jit(solution)/shard_map/ppermute | solution.py:61
  13.3 0.7 copy-start.3
  14.1 0.7 copy-start.4
  45.4 5.5 %copy-start.1 = (bf16[2,128,128]{2,1,0:T(8,128)(2,1)S(1)}, bf16[2,128,128]{2,1,0:T(8,128)(2,1)}, u32[]{:S(2)}) copy-start(bf16[2,128,128]{2,1,0:T(8,128)(2,1)} %param.20) | copy-start | bytes 196612
  51.7 0.7 copy-start.7
  54.5 8.6 %copy-start.6 = (u32[32]{0:T(128)S(1)}, u32[32]{0:T(128)}, u32[]{:S(2)}) copy-start(u32[32]{0:T(128)} %constant.405) | copy-start | bytes 388
  69.6 4.1 %collective-permute-start.3 = (s32[1,16]{1,0:T(1,128)S(1)}, s32[1,16]{1,0:T(1,128)S(1)}, u32[]{:S(2)}, u32[]{:S(2)}) collective-permute-start(s32[1,16]{1,0:T(1,128)S(1)} %collective-permute-done.2), channel_id=1, source_target_pairs={{0,7},{1,0},{2,1},{3,2},{4,3},{5,4},{6,5},{7,6},{8,15},{9,8},{10,9... | collective-permute-start | bytes 200 | tf_op jit(solution)/shard_map/ppermute | solution.py:61
  73.7 6.3 %collective-permute-start.4 = (s32[1,16]{1,0:T(1,128)S(1)}, s32[1,16]{1,0:T(1,128)S(1)}, u32[]{:S(2)}, u32[]{:S(2)}) collective-permute-start(s32[1,16]{1,0:T(1,128)S(1)} %collective-permute-done.3), channel_id=1, source_target_pairs={{0,7},{1,0},{2,1},{3,2},{4,3},{5,4},{6,5},{7,6},{8,15},{9,8},{10,9... | collective-permute-start | bytes 200 | tf_op jit(solution)/shard_map/ppermute | solution.py:61
  79.9 6.3 %collective-permute-start.5 = (s32[1,16]{1,0:T(1,128)S(1)}, s32[1,16]{1,0:T(1,128)S(1)}, u32[]{:S(2)}, u32[]{:S(2)}) collective-permute-start(s32[1,16]{1,0:T(1,128)S(1)} %collective-permute-done.4), channel_id=1, source_target_pairs={{0,7},{1,0},{2,1},{3,2},{4,3},{5,4},{6,5},{7,6},{8,15},{9,8},{10,9... | collective-permute-start | bytes 200 | tf_op jit(solution)/shard_map/ppermute | solution.py:61
  86.2 6.3 %collective-permute-start.6 = (s32[1,16]{1,0:T(1,128)S(1)}, s32[1,16]{1,0:T(1,128)S(1)}, u32[]{:S(2)}, u32[]{:S(2)}) collective-permute-start(s32[1,16]{1,0:T(1,128)S(1)} %collective-permute-done.5), channel_id=1, source_target_pairs={{0,7},{1,0},{2,1},{3,2},{4,3},{5,4},{6,5},{7,6},{8,15},{9,8},{10,9... | collective-permute-start | bytes 200 | tf_op jit(solution)/shard_map/ppermute | solution.py:61
  92.5 6.3 %collective-permute-start.7 = (s32[1,16]{1,0:T(1,128)S(1)}, s32[1,16]{1,0:T(1,128)S(1)}, u32[]{:S(2)}, u32[]{:S(2)}) collective-permute-start(s32[1,16]{1,0:T(1,128)S(1)} %collective-permute-done.6), channel_id=1, source_target_pairs={{0,7},{1,0},{2,1},{3,2},{4,3},{5,4},{6,5},{7,6},{8,15},{9,8},{10,9... | collective-permute-start | bytes 200 | tf_op jit(solution)/shard_map/ppermute | solution.py:61
  97.5 7.6 %copy-start.5 = (s32[1,16]{1,0:T(1,128)S(1)}, s32[1,16]{1,0:T(1,128)}, u32[]{:S(2)}) copy-start(s32[1,16]{1,0:T(1,128)} %param.18) | copy-start | bytes 196
  98.7 6.3 %collective-permute-start.8 = (s32[1,16]{1,0:T(1,128)S(1)}, s32[1,16]{1,0:T(1,128)S(1)}, u32[]{:S(2)}, u32[]{:S(2)}) collective-permute-start(s32[1,16]{1,0:T(1,128)S(1)} %collective-permute-done.7), channel_id=1, source_target_pairs={{0,7},{1,0},{2,1},{3,2},{4,3},{5,4},{6,5},{7,6},{8,15},{9,8},{10,9... | collective-permute-start | bytes 200 | tf_op jit(solution)/shard_map/ppermute | solution.py:61
  193.4 3.7 %collective-permute-start = (bf16[8,16,128]{2,1,0:T(8,128)(2,1)S(1)}, bf16[8,16,128]{2,1,0:T(8,128)(2,1)S(1)}, u32[]{:S(2)}, u32[]{:S(2)}) collective-permute-start(bf16[8,16,128]{2,1,0:T(8,128)(2,1)S(1)} %copy.33), channel_id=1, source_target_pairs={{0,8},{8,16},{16,24},{24,0},{1,9},{9,17},{17,25},{25,1},{2,10},{10... | collective-permute-start | bytes 98312 | tf_op jit(solution)/shard_map/while/body/eval_jaxpr/ppermute | solution.py:25
  194.3 3.7 %collective-permute-start.1 = (f32[8,16,128]{2,1,0:T(8,128)S(1)}, f32[8,16,128]{2,1,0:T(8,128)S(1)}, u32[]{:S(2)}, u32[]{:S(2)}) collective-permute-start(f32[8,16,128]{2,1,0:T(8,128)S(1)} %add.317), channel_id=1, source_target_pairs={{0,8},{8,16},{16,24},{24,0},{1,9},{9,17},{17,25},{25,1},{2,10},{10... | collective-permute-start | bytes 196616 | tf_op jit(solution)/shard_map/while/body/eval_jaxpr/ppermute | solution.py:25
  198.1 3.7 %collective-permute-start = (bf16[8,16,128]{2,1,0:T(8,128)(2,1)S(1)}, bf16[8,16,128]{2,1,0:T(8,128)(2,1)S(1)}, u32[]{:S(2)}, u32[]{:S(2)}) collective-permute-start(bf16[8,16,128]{2,1,0:T(8,128)(2,1)S(1)} %copy.33), channel_id=1, source_target_pairs={{0,8},{8,16},{16,24},{24,0},{1,9},{9,17},{17,25},{25,1},{2,10},{10... | collective-permute-start | bytes 98312 | tf_op jit(solution)/shard_map/while/body/eval_jaxpr/ppermute | solution.py:25
  199.0 3.7 %collective-permute-start.1 = (f32[8,16,128]{2,1,0:T(8,128)S(1)}, f32[8,16,128]{2,1,0:T(8,128)S(1)}, u32[]{:S(2)}, u32[]{:S(2)}) collective-permute-start(f32[8,16,128]{2,1,0:T(8,128)S(1)} %add.317), channel_id=1, source_target_pairs={{0,8},{8,16},{16,24},{24,0},{1,9},{9,17},{17,25},{25,1},{2,10},{10... | collective-permute-start | bytes 196616 | tf_op jit(solution)/shard_map/while/body/eval_jaxpr/ppermute | solution.py:25
  202.7 3.6 %collective-permute-start = (bf16[8,16,128]{2,1,0:T(8,128)(2,1)S(1)}, bf16[8,16,128]{2,1,0:T(8,128)(2,1)S(1)}, u32[]{:S(2)}, u32[]{:S(2)}) collective-permute-start(bf16[8,16,128]{2,1,0:T(8,128)(2,1)S(1)} %copy.33), channel_id=1, source_target_pairs={{0,8},{8,16},{16,24},{24,0},{1,9},{9,17},{17,25},{25,1},{2,10},{10... | collective-permute-start | bytes 98312 | tf_op jit(solution)/shard_map/while/body/eval_jaxpr/ppermute | solution.py:25
  203.6 3.7 %collective-permute-start.1 = (f32[8,16,128]{2,1,0:T(8,128)S(1)}, f32[8,16,128]{2,1,0:T(8,128)S(1)}, u32[]{:S(2)}, u32[]{:S(2)}) collective-permute-start(f32[8,16,128]{2,1,0:T(8,128)S(1)} %add.317), channel_id=1, source_target_pairs={{0,8},{8,16},{16,24},{24,0},{1,9},{9,17},{17,25},{25,1},{2,10},{10... | collective-permute-start | bytes 196616 | tf_op jit(solution)/shard_map/while/body/eval_jaxpr/ppermute | solution.py:25
  208.0 3.7 %collective-permute-start.9 = (f32[8,16,128]{2,1,0:T(8,128)S(1)}, f32[8,16,128]{2,1,0:T(8,128)S(1)}, u32[]{:S(2)}, u32[]{:S(2)}) collective-permute-start(f32[8,16,128]{2,1,0:T(8,128)S(1)} %add.262), channel_id=1, source_target_pairs={{0,8},{8,16},{16,24},{24,0},{1,9},{9,17},{17,25},{25,1},{2,10},{10... | collective-permute-start | bytes 196616 | tf_op jit(solution)/shard_map/ppermute | solution.py:25
  211.7 0.6 copy-start.2
  212.5 63.4 %copy-start = (f32[2,128,128]{2,1,0:T(8,128)}, f32[2,128,128]{2,1,0:T(8,128)S(1)}, u32[]{:S(2)}) copy-start(f32[2,128,128]{2,1,0:T(8,128)S(1)} %fusion.38) | copy-start | bytes 393220
Sparse Core Ops, SparseCore 0:
  212.5 63.4 reduce-scatter.1
